TPU v7x, 32 devices: a whole 2x2x4 slice. The times are simulated.
32 devices in a mesh: ctx: 8 (over y, x, core), tp: 4 (over z).
Axes of the slice: x: 2, y: 2, z: 4, core: 2. Of those that a mesh axis runs over, the one named last changes fastest.
Arguments:
- tokens: bfloat16 [4096, 4096], P('ctx', 'tp'), may hold values from -6 to 6
- norm_gain: float32 [4096], replicated, may hold values from 0.5 to 1.5
- proj_weight: bfloat16 [3, 4096, 2048], P(None, None, 'tp'), may hold values from -0.09375 to 0.09375
- short_taps: float32 [3, 3, 2048], P(None, None, 'tp'), may hold values from -1 to 1
- long_filter: float32 [4096, 2048], P('ctx', 'tp'), may hold values from -0.09375 to 0.09375
- skip_gain: float32 [2048], P('tp'), may hold values from -1 to 1
Outputs:
- output: bfloat16 [4096, 2048], P('ctx', 'tp')
All inputs are finite; a program needn't handle non-finite values.
Results may differ from a plain program's by a relative error of at most 0.0081.
Values may be sent and summed in bfloat16 or wider, within the bound.
A program may use at most 128 MiB of HBM per device.

v0:
```python
import math
import jax
import jax.numpy as jnp
from jax import lax
from jax.sharding import PartitionSpec as P

highest = lax.Precision.HIGHEST


def from_behind(array, axis, by):
    devices = lax.axis_size(axis)
    pairs = [(i, i + by) for i in range(devices) if 0 <= i + by < devices]
    return lax.ppermute(array, axis, pairs)


def outer_tables(part_count):
    frequency = jnp.arange(2 * part_count, dtype=jnp.int32)
    source = jnp.arange(part_count, dtype=jnp.int32)
    turn_count = frequency[:, None] * source[None, :] % (2 * part_count)
    angles = turn_count.astype(jnp.float32) * (math.pi / part_count)
    return (jnp.cos(angles), jnp.sin(angles))


def inner_tables(row_count):
    step_index = jnp.arange(row_count, dtype=jnp.int32)
    turn_count = step_index[:, None] * step_index[None, :] % row_count
    angles = turn_count.astype(jnp.float32) * (2.0 * math.pi / row_count)
    return (jnp.cos(angles), jnp.sin(angles))


def twist_tables(own_index, part_count, block_rows, total_length):
    frequency = jnp.arange(2 * part_count, dtype=jnp.int32)
    column = own_index * block_rows + jnp.arange(block_rows, dtype=jnp.int32)
    turn_count = frequency[:, None] * column[None, :] % total_length
    angles = turn_count.astype(jnp.float32) * (2.0 * math.pi / total_length)
    return (jnp.cos(angles)[:, :, None], jnp.sin(angles)[:, :, None])


def forward_transform(signal, part_count, tables, regroup, spread):
    outer_cos, outer_sin, inner_cos, inner_sin, twist_cos, twist_sin = tables
    row_count, width_all = signal.shape
    block_rows = row_count // part_count
    regrouped = regroup(signal).reshape(part_count, block_rows, width_all)
    outer_real = jnp.einsum("an,njw->ajw", outer_cos, regrouped, precision=highest)
    outer_imag = -jnp.einsum("an,njw->ajw", outer_sin, regrouped, precision=highest)
    turned_real = outer_real * twist_cos + outer_imag * twist_sin
    turned_imag = outer_imag * twist_cos - outer_real * twist_sin
    arrived = spread(jnp.stack([turned_real, turned_imag]))
    spec_real = jnp.einsum("bj,ejw->ebw", inner_cos, arrived[0], precision=highest) + jnp.einsum(
        "bj,ejw->ebw", inner_sin, arrived[1], precision=highest
    )
    spec_imag = jnp.einsum("bj,ejw->ebw", inner_cos, arrived[1], precision=highest) - jnp.einsum(
        "bj,ejw->ebw", inner_sin, arrived[0], precision=highest
    )
    return (spec_real, spec_imag)


def inverse_transform(spec_real, spec_imag, part_count, tables):
    outer_cos, outer_sin, inner_cos, inner_sin, twist_cos, twist_sin = tables
    row_count = spec_real.shape[1]
    width_all = spec_real.shape[2]
    back_real = jnp.einsum("jb,ebw->ejw", inner_cos, spec_real, precision=highest) - jnp.einsum(
        "jb,ebw->ejw", inner_sin, spec_imag, precision=highest
    )
    back_imag = jnp.einsum("jb,ebw->ejw", inner_sin, spec_real, precision=highest) + jnp.einsum(
        "jb,ebw->ejw", inner_cos, spec_imag, precision=highest
    )
    arrived = lax.all_to_all(
        jnp.stack([back_real, back_imag]), "ctx", split_axis=2, concat_axis=1, tiled=True
    )
    turned_real = arrived[0] * twist_cos - arrived[1] * twist_sin
    turned_imag = arrived[0] * twist_sin + arrived[1] * twist_cos
    total_length = 2 * row_count * part_count
    folded = (
        jnp.einsum("an,ajw->njw", outer_cos, turned_real, precision=highest)
        - jnp.einsum("an,ajw->njw", outer_sin, turned_imag, precision=highest)
    ) / total_length
    return lax.all_to_all(
        folded.reshape(row_count, width_all), "ctx", split_axis=0, concat_axis=0, tiled=True
    )


def body(tokens, norm_gain, proj_weight, short_taps, long_filter, skip_gain):
    gathered = lax.all_gather(tokens, "tp", axis=1, tiled=True)
    widened = gathered.astype(jnp.float32)
    scaling = lax.rsqrt(jnp.mean(widened * widened, axis=1, keepdims=True) + 1e-06)
    normed = (widened * scaling * norm_gain).astype(jnp.bfloat16)
    projected = jnp.einsum(
        "td,bdc->btc", normed, proj_weight, preferred_element_type=jnp.float32
    ).astype(jnp.bfloat16)
    previous = from_behind(projected[:, -2:, :], "ctx", 1)
    extended = jnp.concatenate([previous, projected], axis=1).astype(jnp.float32)
    branch = (
        short_taps[:, 0, None, :] * extended[:, 2:, :]
        + short_taps[:, 1, None, :] * extended[:, 1:-1, :]
        + short_taps[:, 2, None, :] * extended[:, :-2, :]
    )
    mixed_field = branch[1] * branch[2]
    row_count, channels = mixed_field.shape
    part_count = lax.axis_size("ctx")
    own_index = lax.axis_index("ctx")
    block_rows = row_count // part_count
    total_length = 2 * row_count * part_count
    outer_cos, outer_sin = outer_tables(part_count)
    inner_cos, inner_sin = inner_tables(row_count)
    twist_cos, twist_sin = twist_tables(own_index, part_count, block_rows, total_length)
    tables = (outer_cos, outer_sin, inner_cos, inner_sin, twist_cos, twist_sin)
    gain_real, gain_imag = forward_transform(
        long_filter,
        part_count,
        tables,
        lambda values: lax.all_to_all(values, "ctx", split_axis=0, concat_axis=0, tiled=True),
        lambda values: lax.all_to_all(
            values.astype(jnp.bfloat16), "ctx", split_axis=1, concat_axis=2, tiled=True
        ).astype(values.dtype),
    )
    data_real, data_imag = forward_transform(
        mixed_field,
        part_count,
        tables,
        lambda values: lax.all_to_all(values, "ctx", split_axis=0, concat_axis=0, tiled=True),
        lambda values: lax.all_to_all(
            values.astype(jnp.bfloat16), "ctx", split_axis=1, concat_axis=2, tiled=True
        ).astype(values.dtype),
    )
    product_real = data_real * gain_real - data_imag * gain_imag
    product_imag = data_real * gain_imag + data_imag * gain_real
    convolved = inverse_transform(product_real, product_imag, part_count, tables)
    return (branch[0] * (convolved + skip_gain * mixed_field)).astype(jnp.bfloat16)


def solution(mesh):
    placed = (
        P("ctx", "tp"),
        P(),
        P(None, None, "tp"),
        P(None, None, "tp"),
        P("ctx", "tp"),
        P("tp"),
    )
    return jax.shard_map(
        body, mesh=mesh, in_specs=placed, out_specs=P("ctx", "tp"), check_vma=False
    )
```

profile of v0, /device:TPU:0, one launch (start us, length us, event | category | flops | bytes accessed | tf_op | source)
XLA Modules:
  0.0 390.0 jit_solution(1918648023505237398)
XLA Ops:
  7.3 5.2 %all-to-all-start.2 = ((f32[8,64,512]{2,1,0:T(8,128)}), f32[8,64,512]{2,1,0:T(8,128)}, u32[]{:S(2)}, u32[]{:S(2)}) async-start(f32[8,64,512]{2,1,0:T(8,128)} %bitcast.138), calls=%async_computation.2 | async-start | bytes 2097152 | tf_op jit(solution)/shard_map/all_to_all | solution.py:112
  12.5 79.9 %all-gather.2.cloned.1.call-done = bf16[512,4096]{1,0:T(8,128)(2,1)} async-done(((bf16[512,1024]{1,0:T(8,128)(2,1)}), bf16[512,4096]{1,0:T(8,128)(2,1)}) %all-gather.2.cloned.1.call-update) | async-done | bytes 4194320 | tf_op jit(solution)/shard_map/all_gather | solution.py:84
  95.9 9.9 %fusion.33 = bf16[3,512,512]{2,1,0:T(8,128)(2,1)S(1)} fusion(bf16[3,4096,512]{2,1,0:T(8,128)(2,1)} %param.8, bf16[512,4096]{1,0:T(8,128)(2,1)S(1)} %copy-done.3, f32[4096]{0:T(1024)S(1)} %copy-done.8, f32[512]{0:T(512)S(1)} %add_rsqrt_fusion), kind=kOutput, calls=%fused_computation.50 | convolution fusion | flops 6451625984 | bytes 18368512 | tf_op jit(solution)/shard_map/td,bdc->btc/dot_general | solution.py:88
  110.9 6.6 %all-to-all-start = ((f32[8,64,512]{2,1,0:T(8,128)}), f32[8,64,512]{2,1,0:T(8,128)}, u32[]{:S(2)}, u32[]{:S(2)}) async-start(f32[8,64,512]{2,1,0:T(8,128)} %bitcast.135), calls=%async_computation | async-start | bytes 2097152 | tf_op jit(solution)/shard_map/all_to_all | solution.py:121
  117.7 4.7 %fusion.75 = f32[16,64,512]{2,0,1:T(8,128)} fusion(f32[8,64,512]{2,1,0:T(8,128)} %all-to-all-done.2), kind=kOutput, calls=%fused_computation.89 | convolution fusion | flops 50333440 | bytes 3145728 | tf_op jit(solution)/shard_map/an,njw->ajw/dot_general | solution.py:45
  122.5 4.8 %fusion.77 = f32[16,64,512]{2,0,1:T(8,128)} fusion(f32[8,64,512]{2,1,0:T(8,128)} %all-to-all-done.2), kind=kOutput, calls=%fused_computation.91 | convolution fusion | flops 50333440 | bytes 3145728 | tf_op jit(solution)/shard_map/an,njw->ajw/dot_general | solution.py:44
  127.2 5.7 %all-to-all-done = f32[8,64,512]{2,1,0:T(8,128)} async-done(((f32[8,64,512]{2,1,0:T(8,128)}), f32[8,64,512]{2,1,0:T(8,128)}, u32[]{:S(2)}, u32[]{:S(2)}) %all-to-all-start) | async-done | bytes 1048608 | tf_op jit(solution)/shard_map/all_to_all | solution.py:121
  136.5 5.9 %fusion.47 = (bf16[1,16,64,512]{3,1,2,0:T(8,128)(2,1)S(1)}, bf16[1,16,64,512]{3,1,2,0:T(8,128)(2,1)S(1)}, bf16[1,16,64,512]{3,1,2,0:T(8,128)(2,1)}, bf16[1,16,64,512]{3,1,2,0:T(8,128)(2,1)}) fusion(f32[16,64,512]{2,0,1:T(8,128)S(1)} %copy-done.2, f32[16,64,512]{2,0,1:T(8,128)} %fusion.77, f32[16,64]{0,1:T(8,128)S(1)} %get-tuple-element.23, ...), kind=kOutput, calls=%fused_computation.58 | convolution fusion | flops 59770624 | bytes 11542528 | tf_op jit(solution)/shard_map/an,njw->ajw/dot_general | solution.py:44
  153.7 22.4 %all-to-all-done.3 = bf16[2,16,64,512]{3,2,0,1:T(8,128)(2,1)} async-done(((bf16[2,16,64,512]{3,2,0,1:T(8,128)(2,1)}), bf16[2,16,64,512]{3,2,0,1:T(8,128)(2,1)}, u32[]{:S(2)}, u32[]{:S(2)}) %all-to-all-start.3) | async-done | bytes 2097184 | tf_op jit(solution)/shard_map/all_to_all | solution.py:113
  182.9 6.9 %fusion.64 = f32[2,512,512]{2,1,0:T(8,128)S(1)} fusion(bf16[2,512,512]{2,1,0:T(8,128)(2,1)S(1)} %bitcast.141), kind=kOutput, calls=%fused_computation.78 | convolution fusion | flops 3224895488 | bytes 3145728 | tf_op jit(solution)/shard_map/bj,ejw->ebw/dot_general | solution.py:49
  189.8 6.9 %fusion.60 = f32[2,512,512]{2,1,0:T(8,128)S(1)} fusion(bf16[2,512,512]{2,1,0:T(8,128)(2,1)S(1)} %bitcast.139), kind=kOutput, calls=%fused_computation.74 | convolution fusion | flops 3224895488 | bytes 3145728 | tf_op jit(solution)/shard_map/bj,ejw->ebw/dot_general | solution.py:52
  196.8 7.4 %convolution_add_fusion = f32[2,512,512]{2,1,0:T(8,128)} fusion(f32[2,512,512]{2,1,0:T(8,128)S(1)} %fusion.64, bf16[2,512,512]{2,1,0:T(8,128)(2,1)S(1)} %bitcast.140), kind=kOutput, calls=%fused_computation.44 | convolution fusion | flops 3225419776 | bytes 5242880 | tf_op jit(solution)/shard_map/bj,ejw->ebw/dot_general | solution.py:49
  204.2 7.6 %convolution_subtract_fusion = f32[2,512,512]{2,1,0:T(8,128)} fusion(f32[2,512,512]{2,1,0:T(8,128)S(1)} %fusion.60, bf16[2,512,512]{2,1,0:T(8,128)(2,1)S(1)} %bitcast.142), kind=kOutput, calls=%fused_computation.42 | convolution fusion | flops 3225419776 | bytes 5242880 | tf_op jit(solution)/shard_map/bj,ejw->ebw/dot_general | solution.py:52
  214.0 6.9 %fusion.62 = f32[2,512,512]{2,1,0:T(8,128)S(1)} fusion(bf16[2,512,512]{2,1,0:T(8,128)(2,1)S(1)} %bitcast.143), kind=kOutput, calls=%fused_computation.76 | convolution fusion | flops 3224895488 | bytes 3145728 | tf_op jit(solution)/shard_map/bj,ejw->ebw/dot_general | solution.py:52
  220.9 6.9 %fusion.66 = f32[2,512,512]{2,1,0:T(8,128)S(1)} fusion(bf16[2,512,512]{2,1,0:T(8,128)(2,1)S(1)} %bitcast.136), kind=kOutput, calls=%fused_computation.80 | convolution fusion | flops 3224895488 | bytes 3145728 | tf_op jit(solution)/shard_map/bj,ejw->ebw/dot_general | solution.py:49
  227.9 7.4 %convolution_add_fusion.1 = f32[2,512,512]{2,1,0:T(8,128)S(1)} fusion(f32[2,512,512]{2,1,0:T(8,128)S(1)} %fusion.66, bf16[2,512,512]{2,1,0:T(8,128)(2,1)S(1)} %bitcast.144), kind=kOutput, calls=%fused_computation.45 | convolution fusion | flops 3225419776 | bytes 5242880 | tf_op jit(solution)/shard_map/bj,ejw->ebw/dot_general | solution.py:49
  235.3 7.5 %multiply_subtract_fusion = (f32[2,512,512]{2,1,0:T(8,128)S(1)}, f32[2,512,512]{2,1,0:T(8,128)S(1)}) fusion(f32[2,512,512]{2,1,0:T(8,128)S(1)} %copy-done.5, f32[2,512,512]{2,1,0:T(8,128)S(1)} %convolution_add_fusion.1, f32[2,512,512]{2,1,0:T(8,128)S(1)} %copy-done.4, f32[2,512,512]{2,1,0:T(8,128)S(1)} %fusion.62, bf16[2,512,512]{2,1,0:T(8,128)(2,1)S(1)} %bitcast.137), kind=kOutput, calls=%fused_computation.36 | convolution fusion | flops 3228565504 | bytes 13631488 | tf_op jit(solution)/shard_map/bj,ejw->ebw/dot_general | solution.py:52
  242.8 8.4 %fusion.10 = f32[2,512,512]{2,1,0:T(8,128)S(1)} fusion(f32[2,512,512]{2,1,0:T(8,128)S(1)} %get-tuple-element.6), kind=kOutput, calls=%fused_computation.17 | convolution fusion | flops 3224895488 | bytes 4194304 | tf_op jit(solution)/shard_map/jb,ebw->ejw/dot_general | solution.py:65
  251.2 8.6 %fusion.12 = f32[2,512,512]{2,1,0:T(8,128)S(1)} fusion(f32[2,512,512]{2,1,0:T(8,128)S(1)} %get-tuple-element.6), kind=kOutput, calls=%fused_computation.19 | convolution fusion | flops 3224895488 | bytes 4194304 | tf_op jit(solution)/shard_map/jb,ebw->ejw/dot_general | solution.py:62
  259.8 8.5 %subtract_bitcast_fusion = f32[1,2,512,512]{2,3,1,0:T(8,128)S(1)} fusion(f32[2,512,512]{2,1,0:T(8,128)S(1)} %fusion.12, f32[2,512,512]{2,1,0:T(8,128)S(1)} %get-tuple-element.5), kind=kOutput, calls=%fused_computation.34 | convolution fusion | flops 3225419776 | bytes 6291456 | tf_op jit(solution)/shard_map/jb,ebw->ejw/dot_general | solution.py:62
  268.3 8.5 %add_bitcast_fusion = f32[1,2,512,512]{2,3,1,0:T(8,128)S(1)} fusion(f32[2,512,512]{2,1,0:T(8,128)S(1)} %fusion.10, f32[2,512,512]{2,1,0:T(8,128)S(1)} %get-tuple-element.5), kind=kOutput, calls=%fused_computation.33 | convolution fusion | flops 3225419776 | bytes 6291456 | tf_op jit(solution)/shard_map/jb,ebw->ejw/dot_general | solution.py:65
  279.1 7.3 %copy.69 = f32[2,2,512,512]{3,1,0,2:T(2,128)} copy(f32[2,2,512,512]{2,3,1,0:T(8,128)} %pad_maximum_fusion) | data formatting | bytes 8388608 | tf_op jit(solution)/shard_map/stack | solution.py:69
  286.4 53.4 %all_to_all.69 = f32[2,2,512,512]{3,1,0,2:T(2,128)S(1)} all-to-all(f32[2,2,512,512]{3,1,0,2:T(2,128)} %copy.69), channel_id=1, replica_groups=mesh['ctx'=8,'tp'=4] {'ctx'}, dimensions={2} | all-to-all | bytes 8388608 | tf_op jit(solution)/shard_map/all_to_all | solution.py:68
  363.8 17.8 %all_to_all.70 = f32[8,64,512]{2,1,0:T(8,128)S(1)} all-to-all(f32[8,64,512]{2,1,0:T(8,128)S(1)} %copy.73), channel_id=1, replica_groups=mesh['ctx'=8,'tp'=4] {'ctx'}, dimensions={0} | all-to-all | bytes 2097152 | tf_op jit(solution)/shard_map/all_to_all | solution.py:78
  (61 shorter events, 60.9 us)
Async XLA Ops:
  6.5 5.9 %copy-start.6 = (f32[3,3,512]{2,1,0:T(4,128)S(1)}, f32[3,3,512]{2,1,0:T(4,128)}, u32[]{:S(2)}) copy-start(f32[3,3,512]{2,1,0:T(4,128)} %param.9) | copy-start | bytes 55300
  6.5 85.9 %all-gather.2.cloned.1.call-start = ((), (), s32[]{:S(2)}) async-start(), calls=%async_computation.6 | async-start | bytes 5242880 | tf_op jit(solution)/shard_map/all_gather | solution.py:84
  7.3 103.7 %all-to-all-start.2 = ((f32[8,64,512]{2,1,0:T(8,128)}), f32[8,64,512]{2,1,0:T(8,128)}, u32[]{:S(2)}, u32[]{:S(2)}) async-start(f32[8,64,512]{2,1,0:T(8,128)} %bitcast.138), calls=%async_computation.2 | async-start | bytes 2097152 | tf_op jit(solution)/shard_map/all_to_all | solution.py:112
  12.4 83.2 %copy-start.8 = (f32[4096]{0:T(1024)S(1)}, f32[4096]{0:T(1024)}, u32[]{:S(2)}) copy-start(f32[4096]{0:T(1024)} %param.7) | copy-start | bytes 49156
  92.4 3.4 copy-start.3
  105.8 2.6 collective-permute-start
  110.9 22.0 %all-to-all-start = ((f32[8,64,512]{2,1,0:T(8,128)}), f32[8,64,512]{2,1,0:T(8,128)}, u32[]{:S(2)}, u32[]{:S(2)}) async-start(f32[8,64,512]{2,1,0:T(8,128)} %bitcast.135), calls=%async_computation | async-start | bytes 2097152 | tf_op jit(solution)/shard_map/all_to_all | solution.py:121
  132.9 3.6 copy-start.2
  145.2 31.0 %all-to-all-start.3 = ((bf16[2,16,64,512]{3,2,0,1:T(8,128)(2,1)}), bf16[2,16,64,512]{3,2,0,1:T(8,128)(2,1)}, u32[]{:S(2)}, u32[]{:S(2)}) async-start(bf16[2,16,64,512]{3,2,0,1:T(8,128)(2,1)} %copy.59), calls=%async_computation.3 | async-start | bytes 4194304 | tf_op jit(solution)/shard_map/all_to_all | solution.py:113
  176.2 35.6 %all-to-all-start.1 = ((bf16[2,16,64,512]{3,2,0,1:T(8,128)(2,1)}), bf16[2,16,64,512]{3,2,0,1:T(8,128)(2,1)}, u32[]{:S(2)}, u32[]{:S(2)}) async-start(bf16[2,16,64,512]{3,2,0,1:T(8,128)(2,1)} %copy.51), calls=%async_computation.1 | async-start | bytes 4194304 | tf_op jit(solution)/shard_map/all_to_all | solution.py:122
  227.8 7.4 %copy-start.4 = (f32[2,512,512]{2,1,0:T(8,128)S(1)}, f32[2,512,512]{2,1,0:T(8,128)}, u32[]{:S(2)}) copy-start(f32[2,512,512]{2,1,0:T(8,128)} %convolution_add_fusion) | copy-start | bytes 6291460
  227.8 7.4 %copy-start.5 = (f32[2,512,512]{2,1,0:T(8,128)S(1)}, f32[2,512,512]{2,1,0:T(8,128)}, u32[]{:S(2)}) copy-start(f32[2,512,512]{2,1,0:T(8,128)} %convolution_subtract_fusion) | copy-start | bytes 6291460
  358.0 3.8 copy-start
  358.0 3.8 copy-start.1
  363.2 18.4 %copy-start.7 = (f32[512]{0:T(512)S(1)}, f32[512]{0:T(512)}, u32[]{:S(2)}) copy-start(f32[512]{0:T(512)} %param.11) | copy-start | bytes 6148
Sparse Core Ops, SparseCore 0:
  8.9 83.4 all-gather.1
where the time goes:
time: 395 us; the launch traced here: 390 us
  matrix products  126 us (32%)
  waiting for transfers between devices  110 us (28%)
  blocking collectives  71.2 us (18%)
  local copies, waits for them, and re-layouts  35.7 us (9%)
  starting transfers between devices  22.4 us (6%)
  between operations  14 us (4%)
  other arithmetic  11.6 us (3%)
    all_gather x1, waiting for transfers between devices, body(): gathered = lax.all_gather(tokens, 'tp', axis=1, tiled=True)  79.9 us
    all_to_all x1, blocking collectives, inverse_transform(): lax.all_to_all(jnp.stack([back_real, back_imag]), 'ctx', split_axis=2, co...  53.4 us
    all_to_all x2, waiting for transfers between devices, body(): lax.all_to_all(values.astype(jnp.bfloat16), 'ctx', split_axis=1, concat_a...  22.4 us
    all_to_all x1, blocking collectives, inverse_transform(): lax.all_to_all(folded.reshape(row_count, width_all), 'ctx', split_axis=0,...  17.8 us
    dot_general x2, matrix products, forward_transform(): jnp.einsum('bj,ejw->ebw', inner_sin, arrived[0], precision=highest)  15.1 us
    dot_general x2, matrix products, forward_transform(): jnp.einsum('bj,ejw->ebw', inner_sin, arrived[1], precision=highest)  14.8 us
    dot_general x2, matrix products, forward_transform(): jnp.einsum('bj,ejw->ebw', inner_cos, arrived[0], precision=highest)  13.8 us
    dot_general x2, matrix products, forward_transform(): jnp.einsum('bj,ejw->ebw', inner_cos, arrived[1], precision=highest)  13.8 us
  transfers between devices with their start and end apart: 6, of which 4 were waited for; matrix products, arithmetic and copies ran while one was open for 16% of the time, Pallas kernels for 0%

commit v1 on v0

--- a/solution.py
+++ b/solution.py
@@ -65,8 +65,14 @@
     back_imag = jnp.einsum("jb,ebw->ejw", inner_sin, spec_real, precision=highest) + jnp.einsum(
         "jb,ebw->ejw", inner_cos, spec_imag, precision=highest
     )
-    arrived = lax.all_to_all(
-        jnp.stack([back_real, back_imag]), "ctx", split_axis=2, concat_axis=1, tiled=True
+    arrived = jnp.concatenate(
+        lax.all_to_all(
+            jnp.stack(jnp.split(jnp.stack([back_real, back_imag]), lax.axis_size("ctx"), axis=2)),
+            "ctx",
+            0,
+            0,
+        ),
+        axis=1,
     )
     turned_real = arrived[0] * twist_cos - arrived[1] * twist_sin
     turned_imag = arrived[0] * twist_sin + arrived[1] * twist_cos

time: 395 us -> 365 us (0.924)
  local copies, waits for them, and re-layouts: 35.7 us -> 10.9 us
    slice x3 -> x1, local copies, waits for them, and re-layouts: 9.5 us -> 0.7 us  [inverse_transform(): turned_real = arrived[0] * twist_cos - arrived[1] * twist_sin]
    another operation x1 -> x0, local copies, waits for them, and re-layouts: 7.32 us -> none  [inverse_transform(): jnp.stack([back_real, back_imag])]
    squeeze x2 -> x0, local copies, waits for them, and re-layouts: 7.28 us -> none  [inverse_transform(): turned_real = arrived[0] * twist_cos - arrived[1] * twist_sin]
  transfers between devices with their start and end apart: 6 -> 6, of which waited for: 4 -> 4; matrix products, arithmetic and copies ran while one was open for 16% -> 17% of each run, Pallas kernels for 0% -> 0%
where the time goes in v1:
time: 365 us; the launch traced here: 360 us
  matrix products  123 us (34%)
  waiting for transfers between devices  110 us (30%)
  blocking collectives  70.8 us (19%)
  starting transfers between devices  22.2 us (6%)
  between operations  14 us (4%)
  local copies, waits for them, and re-layouts  10.9 us (3%)
  other arithmetic  9.56 us (3%)
    all_gather x1, waiting for transfers between devices, body(): gathered = lax.all_gather(tokens, 'tp', axis=1, tiled=True)  79.9 us
    all_to_all x1, blocking collectives, inverse_transform(): lax.all_to_all(jnp.stack(jnp.split(jnp.stack([back_real, back_imag]), lax...  53 us
    all_to_all x2, waiting for transfers between devices, body(): lax.all_to_all(values.astype(jnp.bfloat16), 'ctx', split_axis=1, concat_a...  22.4 us
    all_to_all x1, blocking collectives, inverse_transform(): lax.all_to_all(folded.reshape(row_count, width_all), 'ctx', split_axis=0,...  17.8 us
    dot_general x2, matrix products, forward_transform(): jnp.einsum('bj,ejw->ebw', inner_sin, arrived[0], precision=highest)  15.5 us
    dot_general x2, matrix products, forward_transform(): jnp.einsum('bj,ejw->ebw', inner_sin, arrived[1], precision=highest)  14.6 us
    dot_general x2, matrix products, forward_transform(): jnp.einsum('bj,ejw->ebw', inner_cos, arrived[0], precision=highest)  13.8 us
    dot_general x2, matrix products, forward_transform(): jnp.einsum('bj,ejw->ebw', inner_cos, arrived[1], precision=highest)  13.8 us
  transfers between devices with their start and end apart: 6, of which 4 were waited for; matrix products, arithmetic and copies ran while one was open for 17% of the time, Pallas kernels for 0%

profile of v1, /device:TPU:0, one launch (start us, length us, event | category | flops | bytes accessed | tf_op | source)
XLA Modules:
  0.0 360.3 jit_solution(16365154678100561915)
XLA Ops:
  7.3 5.2 %all-to-all-start.2 = ((f32[8,64,512]{2,1,0:T(8,128)}), f32[8,64,512]{2,1,0:T(8,128)}, u32[]{:S(2)}, u32[]{:S(2)}) async-start(f32[8,64,512]{2,1,0:T(8,128)} %bitcast.170), calls=%async_computation.2 | async-start | bytes 2097152 | tf_op jit(solution)/shard_map/all_to_all | solution.py:118
  12.5 79.9 %all-gather.2.cloned.1.call-done = bf16[512,4096]{1,0:T(8,128)(2,1)} async-done(((bf16[512,1024]{1,0:T(8,128)(2,1)}), bf16[512,4096]{1,0:T(8,128)(2,1)}) %all-gather.2.cloned.1.call-update) | async-done | bytes 4194320 | tf_op jit(solution)/shard_map/all_gather | solution.py:90
  95.9 9.9 %fusion.37 = bf16[3,512,512]{2,1,0:T(8,128)(2,1)S(1)} fusion(bf16[3,4096,512]{2,1,0:T(8,128)(2,1)} %param.8, bf16[512,4096]{1,0:T(8,128)(2,1)S(1)} %copy-done.1, f32[4096]{0:T(1024)S(1)} %copy-done.6, f32[512]{0:T(512)S(1)} %add_rsqrt_fusion), kind=kOutput, calls=%fused_computation.67 | convolution fusion | flops 6451625984 | bytes 18368512 | tf_op jit(solution)/shard_map/td,bdc->btc/dot_general | solution.py:94
  110.9 6.3 %all-to-all-start = ((f32[8,64,512]{2,1,0:T(8,128)}), f32[8,64,512]{2,1,0:T(8,128)}, u32[]{:S(2)}, u32[]{:S(2)}) async-start(f32[8,64,512]{2,1,0:T(8,128)} %bitcast.167), calls=%async_computation | async-start | bytes 2097152 | tf_op jit(solution)/shard_map/all_to_all | solution.py:127
  117.4 4.7 %fusion.79 = f32[16,64,512]{2,0,1:T(8,128)} fusion(f32[8,64,512]{2,1,0:T(8,128)} %all-to-all-done.2), kind=kOutput, calls=%fused_computation.106 | convolution fusion | flops 50333440 | bytes 3145728 | tf_op jit(solution)/shard_map/an,njw->ajw/dot_general | solution.py:45
  122.2 4.8 %fusion.81 = f32[16,64,512]{2,0,1:T(8,128)} fusion(f32[8,64,512]{2,1,0:T(8,128)} %all-to-all-done.2), kind=kOutput, calls=%fused_computation.108 | convolution fusion | flops 50333440 | bytes 3145728 | tf_op jit(solution)/shard_map/an,njw->ajw/dot_general | solution.py:44
  127.0 5.7 %all-to-all-done = f32[8,64,512]{2,1,0:T(8,128)} async-done(((f32[8,64,512]{2,1,0:T(8,128)}), f32[8,64,512]{2,1,0:T(8,128)}, u32[]{:S(2)}, u32[]{:S(2)}) %all-to-all-start) | async-done | bytes 1048608 | tf_op jit(solution)/shard_map/all_to_all | solution.py:127
  136.3 5.9 %fusion.51 = (bf16[1,16,64,512]{3,1,2,0:T(8,128)(2,1)S(1)}, bf16[1,16,64,512]{3,1,2,0:T(8,128)(2,1)S(1)}, bf16[1,16,64,512]{3,1,2,0:T(8,128)(2,1)}, bf16[1,16,64,512]{3,1,2,0:T(8,128)(2,1)}) fusion(f32[16,64,512]{2,0,1:T(8,128)S(1)} %copy-done, f32[16,64,512]{2,0,1:T(8,128)} %fusion.81, f32[16,64]{0,1:T(8,128)S(1)} %get-tuple-element.23, ...), kind=kOutput, calls=%fused_computation.75 | convolution fusion | flops 59770624 | bytes 11542528 | tf_op jit(solution)/shard_map/an,njw->ajw/dot_general | solution.py:44
  153.5 22.4 %all-to-all-done.3 = bf16[2,16,64,512]{3,2,0,1:T(8,128)(2,1)} async-done(((bf16[2,16,64,512]{3,2,0,1:T(8,128)(2,1)}), bf16[2,16,64,512]{3,2,0,1:T(8,128)(2,1)}, u32[]{:S(2)}, u32[]{:S(2)}) %all-to-all-start.3) | async-done | bytes 2097184 | tf_op jit(solution)/shard_map/all_to_all | solution.py:119
  175.9 4.6 %all-to-all-start.1 = ((bf16[2,16,64,512]{3,2,0,1:T(8,128)(2,1)}), bf16[2,16,64,512]{3,2,0,1:T(8,128)(2,1)}, u32[]{:S(2)}, u32[]{:S(2)}) async-start(bf16[2,16,64,512]{3,2,0,1:T(8,128)(2,1)} %copy.61), calls=%async_computation.1 | async-start | bytes 4194304 | tf_op jit(solution)/shard_map/all_to_all | solution.py:128
  182.7 6.9 %fusion.68 = f32[2,512,512]{2,1,0:T(8,128)S(1)} fusion(bf16[2,512,512]{2,1,0:T(8,128)(2,1)S(1)} %bitcast.173), kind=kOutput, calls=%fused_computation.95 | convolution fusion | flops 3224895488 | bytes 3145728 | tf_op jit(solution)/shard_map/bj,ejw->ebw/dot_general | solution.py:49
  189.6 6.9 %fusion.64 = f32[2,512,512]{2,1,0:T(8,128)S(1)} fusion(bf16[2,512,512]{2,1,0:T(8,128)(2,1)S(1)} %bitcast.171), kind=kOutput, calls=%fused_computation.91 | convolution fusion | flops 3224895488 | bytes 3145728 | tf_op jit(solution)/shard_map/bj,ejw->ebw/dot_general | solution.py:52
  196.5 7.4 %convolution_add_fusion = f32[2,512,512]{2,1,0:T(8,128)} fusion(f32[2,512,512]{2,1,0:T(8,128)S(1)} %fusion.68, bf16[2,512,512]{2,1,0:T(8,128)(2,1)S(1)} %bitcast.172), kind=kOutput, calls=%fused_computation.61 | convolution fusion | flops 3225419776 | bytes 5242880 | tf_op jit(solution)/shard_map/bj,ejw->ebw/dot_general | solution.py:49
  203.9 7.8 %convolution_subtract_fusion = f32[2,512,512]{2,1,0:T(8,128)} fusion(f32[2,512,512]{2,1,0:T(8,128)S(1)} %fusion.64, bf16[2,512,512]{2,1,0:T(8,128)(2,1)S(1)} %bitcast.174), kind=kOutput, calls=%fused_computation.59 | convolution fusion | flops 3225419776 | bytes 5242880 | tf_op jit(solution)/shard_map/bj,ejw->ebw/dot_general | solution.py:52
  213.9 6.9 %fusion.66 = f32[2,512,512]{2,1,0:T(8,128)S(1)} fusion(bf16[2,512,512]{2,1,0:T(8,128)(2,1)S(1)} %bitcast.175), kind=kOutput, calls=%fused_computation.93 | convolution fusion | flops 3224895488 | bytes 3145728 | tf_op jit(solution)/shard_map/bj,ejw->ebw/dot_general | solution.py:52
  220.9 6.9 %fusion.70 = f32[2,512,512]{2,1,0:T(8,128)S(1)} fusion(bf16[2,512,512]{2,1,0:T(8,128)(2,1)S(1)} %bitcast.168), kind=kOutput, calls=%fused_computation.97 | convolution fusion | flops 3224895488 | bytes 3145728 | tf_op jit(solution)/shard_map/bj,ejw->ebw/dot_general | solution.py:49
  227.8 7.2 %convolution_add_fusion.1 = f32[2,512,512]{2,1,0:T(8,128)S(1)} fusion(f32[2,512,512]{2,1,0:T(8,128)S(1)} %fusion.70, bf16[2,512,512]{2,1,0:T(8,128)(2,1)S(1)} %bitcast.176), kind=kOutput, calls=%fused_computation.62 | convolution fusion | flops 3225419776 | bytes 5242880 | tf_op jit(solution)/shard_map/bj,ejw->ebw/dot_general | solution.py:49
  235.0 7.7 %multiply_subtract_fusion = (f32[2,512,512]{2,1,0:T(8,128)S(1)}, f32[2,512,512]{2,1,0:T(8,128)S(1)}) fusion(f32[2,512,512]{2,1,0:T(8,128)S(1)} %copy-done.3, f32[2,512,512]{2,1,0:T(8,128)S(1)} %convolution_add_fusion.1, f32[2,512,512]{2,1,0:T(8,128)S(1)} %copy-done.2, f32[2,512,512]{2,1,0:T(8,128)S(1)} %fusion.66, bf16[2,512,512]{2,1,0:T(8,128)(2,1)S(1)} %bitcast.169), kind=kOutput, calls=%fused_computation.49 | convolution fusion | flops 3228565504 | bytes 13631488 | tf_op jit(solution)/shard_map/bj,ejw->ebw/dot_general | solution.py:52
  242.7 7.3 %fusion.10 = f32[2,512,512]{1,2,0:T(8,128)S(1)} fusion(f32[2,512,512]{2,1,0:T(8,128)S(1)} %get-tuple-element.6), kind=kOutput, calls=%fused_computation.30 | convolution fusion | flops 3224895488 | bytes 4194304 | tf_op jit(solution)/shard_map/jb,ebw->ejw/dot_general | solution.py:65
  250.1 7.8 %fusion.12 = f32[2,512,512]{1,2,0:T(8,128)S(1)} fusion(f32[2,512,512]{2,1,0:T(8,128)S(1)} %get-tuple-element.6), kind=kOutput, calls=%fused_computation.32 | convolution fusion | flops 3224895488 | bytes 4194304 | tf_op jit(solution)/shard_map/jb,ebw->ejw/dot_general | solution.py:62
  257.9 7.4 %add_bitcast_fusion = f32[1,2,512,512]{3,2,1,0:T(8,128)S(1)} fusion(f32[2,512,512]{1,2,0:T(8,128)S(1)} %fusion.10, f32[2,512,512]{2,1,0:T(8,128)S(1)} %get-tuple-element.5), kind=kOutput, calls=%fused_computation.46 | convolution fusion | flops 3225419776 | bytes 6291456 | tf_op jit(solution)/shard_map/jb,ebw->ejw/dot_general | solution.py:65
  265.3 7.5 %subtract_bitcast_fusion = f32[1,2,512,512]{3,2,1,0:T(8,128)S(1)} fusion(f32[2,512,512]{1,2,0:T(8,128)S(1)} %fusion.12, f32[2,512,512]{2,1,0:T(8,128)S(1)} %get-tuple-element.5), kind=kOutput, calls=%fused_computation.47 | convolution fusion | flops 3225419776 | bytes 6291456 | tf_op jit(solution)/shard_map/jb,ebw->ejw/dot_general | solution.py:62
  273.2 53.0 %all_to_all.59 = f32[8,2,2,64,512]{4,3,2,1,0:T(8,128)S(1)} all-to-all(f32[8,2,2,64,512]{4,3,2,1,0:T(8,128)S(1)} %fusion.109), channel_id=1, replica_groups=mesh['ctx'=8,'tp'=4] {'ctx'}, dimensions={0} | all-to-all | bytes 8388608 | tf_op jit(solution)/shard_map/all_to_all | solution.py:69
  334.2 17.8 %all_to_all.60 = f32[8,64,512]{2,1,0:T(8,128)S(1)} all-to-all(f32[8,64,512]{2,1,0:T(8,128)S(1)} %copy.85), channel_id=1, replica_groups=mesh['ctx'=8,'tp'=4] {'ctx'}, dimensions={0} | all-to-all | bytes 2097152 | tf_op jit(solution)/shard_map/all_to_all | solution.py:84
  (58 shorter events, 38.3 us)
Async XLA Ops:
  6.5 5.9 %copy-start.4 = (f32[3,3,512]{2,1,0:T(4,128)S(1)}, f32[3,3,512]{2,1,0:T(4,128)}, u32[]{:S(2)}) copy-start(f32[3,3,512]{2,1,0:T(4,128)} %param.9) | copy-start | bytes 55300
  6.5 85.9 %all-gather.2.cloned.1.call-start = ((), (), s32[]{:S(2)}) async-start(), calls=%async_computation.6 | async-start | bytes 5242880 | tf_op jit(solution)/shard_map/all_gather | solution.py:90
  7.3 103.7 %all-to-all-start.2 = ((f32[8,64,512]{2,1,0:T(8,128)}), f32[8,64,512]{2,1,0:T(8,128)}, u32[]{:S(2)}, u32[]{:S(2)}) async-start(f32[8,64,512]{2,1,0:T(8,128)} %bitcast.170), calls=%async_computation.2 | async-start | bytes 2097152 | tf_op jit(solution)/shard_map/all_to_all | solution.py:118
  12.4 83.2 %copy-start.6 = (f32[4096]{0:T(1024)S(1)}, f32[4096]{0:T(1024)}, u32[]{:S(2)}) copy-start(f32[4096]{0:T(1024)} %param.7) | copy-start | bytes 49156
  92.4 3.4 copy-start.1
  105.8 2.6 collective-permute-start
  110.9 21.7 %all-to-all-start = ((f32[8,64,512]{2,1,0:T(8,128)}), f32[8,64,512]{2,1,0:T(8,128)}, u32[]{:S(2)}, u32[]{:S(2)}) async-start(f32[8,64,512]{2,1,0:T(8,128)} %bitcast.167), calls=%async_computation | async-start | bytes 2097152 | tf_op jit(solution)/shard_map/all_to_all | solution.py:127
  132.7 3.6 copy-start
  144.9 31.0 %all-to-all-start.3 = ((bf16[2,16,64,512]{3,2,0,1:T(8,128)(2,1)}), bf16[2,16,64,512]{3,2,0,1:T(8,128)(2,1)}, u32[]{:S(2)}, u32[]{:S(2)}) async-start(bf16[2,16,64,512]{3,2,0,1:T(8,128)(2,1)} %copy.69), calls=%async_computation.3 | async-start | bytes 4194304 | tf_op jit(solution)/shard_map/all_to_all | solution.py:119
  175.9 35.9 %all-to-all-start.1 = ((bf16[2,16,64,512]{3,2,0,1:T(8,128)(2,1)}), bf16[2,16,64,512]{3,2,0,1:T(8,128)(2,1)}, u32[]{:S(2)}, u32[]{:S(2)}) async-start(bf16[2,16,64,512]{3,2,0,1:T(8,128)(2,1)} %copy.61), calls=%async_computation.1 | async-start | bytes 4194304 | tf_op jit(solution)/shard_map/all_to_all | solution.py:128
  227.8 7.2 %copy-start.2 = (f32[2,512,512]{2,1,0:T(8,128)S(1)}, f32[2,512,512]{2,1,0:T(8,128)}, u32[]{:S(2)}) copy-start(f32[2,512,512]{2,1,0:T(8,128)} %convolution_add_fusion) | copy-start | bytes 6291460
  227.8 7.2 %copy-start.3 = (f32[2,512,512]{2,1,0:T(8,128)S(1)}, f32[2,512,512]{2,1,0:T(8,128)}, u32[]{:S(2)}) copy-start(f32[2,512,512]{2,1,0:T(8,128)} %convolution_subtract_fusion) | copy-start | bytes 6291460
  333.6 18.4 %copy-start.5 = (f32[512]{0:T(512)S(1)}, f32[512]{0:T(512)}, u32[]{:S(2)}) copy-start(f32[512]{0:T(512)} %param.11) | copy-start | bytes 6148
Sparse Core Ops, SparseCore 0:
  8.9 83.4 all-gather.1
